TPU v7x, 32 devices: a whole 2x2x4 slice. The times are simulated.
32 devices in a mesh: dp: 8 (over z, x), tensor: 4 (over y, core).
Axes of the slice: x: 2, y: 2, z: 4, core: 2. Of those that a mesh axis runs over, the one named last changes fastest.
Arguments:
- patches: bfloat16 [192, 196, 768], P('dp'), may hold values from -6 to 6
- keep_slots: int32 [192, 98], P('dp'), may hold values from 0 to 195, as said below
- visible_count: int32 [192], P('dp'), may hold values from 39 to 98, as said below
- gain_one: float32 [768], replicated, may hold values from 0.1 to 1.9
- shift_one: float32 [768], replicated, may hold values from -4 to 4
- w_qkv: bfloat16 [3, 768, 768], P(None, None, 'tensor'), may hold values from -0.21875 to 0.21875
- b_qv: float32 [2, 768], P(None, 'tensor'), may hold values from -4 to 4
- w_out: bfloat16 [768, 768], P('tensor'), may hold values from -1.75 to 1.75
- b_out: float32 [768], replicated, may hold values from -4 to 4
- gain_two: float32 [768], replicated, may hold values from 0.1 to 1.9
- shift_two: float32 [768], replicated, may hold values from -4 to 4
- w_fc1: bfloat16 [768, 3072], P(None, 'tensor'), may hold values from -0.21875 to 0.21875
- b_fc1: float32 [3072], P('tensor'), may hold values from -4 to 4
- w_fc2: bfloat16 [3072, 768], P('tensor'), may hold values from -0.109375 to 0.109375
- b_fc2: float32 [768], replicated, may hold values from -4 to 4
- out_grad: bfloat16 [192, 98, 768], P(('dp', 'tensor')), may hold values from -6 to 6
Outputs:
- layer_out: bfloat16 [192, 98, 768], P(('dp', 'tensor'))
- grad_patches: float32 [192, 196, 768], P(('dp', 'tensor'))
- grad_gain_one: float32 [768], replicated
- grad_shift_one: float32 [768], replicated
- grad_w_qkv: float32 [3, 768, 768], P(None, None, 'tensor')
- grad_b_qv: float32 [2, 768], P(None, 'tensor')
- grad_w_out: float32 [768, 768], P('tensor')
- grad_b_out: float32 [768], replicated
- grad_gain_two: float32 [768], replicated
- grad_shift_two: float32 [768], replicated
- grad_w_fc1: float32 [768, 3072], P(None, 'tensor')
- grad_b_fc1: float32 [3072], P('tensor')
- grad_w_fc2: float32 [3072, 768], P('tensor')
- grad_b_fc2: float32 [768], replicated
Inputs may be any that keep to these rules, and one draw needn't show every extreme that they name: `visible_count`: visible patches of each image; in every draw some image has 98 and some has 196 // 5. `keep_slots`: the entries of a row are distinct patch indices of the image; the first visible_count of them are its visible patches, the others are ignored.
All inputs are finite; a program needn't handle non-finite values.
Results may differ from a plain program's by a relative error of at most 0.012.
The roundings to bfloat16 on the way count: a program that leaves them out, or rounds other values in their place, can miss the bound.
Values may be sent and summed in bfloat16 or wider, within the bound.
No kernel may reach another device: no remote copies, remote signals or barrier semaphores. Data moves between devices by JAX's collectives and lax.ppermute only.
A program may use at most 192 MiB of HBM per device.

v0:
```python
import jax
import jax.numpy as jnp
from jax import lax
from jax.sharding import PartitionSpec as P

HD = 64
EPSILON = 1e-06
MASKED = -1000000000.0


def standard(inputs):
    average = jnp.mean(inputs, axis=-1, keepdims=True)
    centered = inputs - average
    spread = jnp.mean(centered * centered, axis=-1, keepdims=True)
    return centered * lax.rsqrt(spread + EPSILON)


def affine_norm(inputs, weights, offsets):
    return standard(inputs) * weights + offsets


def norm_back(inputs, weights, offsets, gradient):
    _, backward = jax.vjp(affine_norm, inputs, weights, offsets)
    return backward(gradient)


def exact_gelu(values):
    return jax.nn.gelu(values, approximate=False)


def shards(
    patches,
    keep_slots,
    visible_count,
    gain_one,
    shift_one,
    w_qkv,
    b_qv,
    w_out,
    b_out,
    gain_two,
    shift_two,
    w_fc1,
    b_fc1,
    w_fc2,
    b_fc2,
    out_grad,
):
    images, slots = keep_slots.shape
    share = images // lax.axis_size("tensor")
    begin = lax.axis_index("tensor") * share
    visible = jnp.arange(slots, dtype=jnp.int32)[None, :] < visible_count[:, None]
    mask_share = lax.dynamic_slice_in_dim(visible, begin, share, 0)[:, :, None].astype(jnp.float32)
    tokens = jnp.take_along_axis(patches, keep_slots[:, :, None], axis=1).astype(jnp.float32)
    token_share = lax.dynamic_slice_in_dim(tokens, begin, share, 0)
    first = affine_norm(tokens, gain_one, shift_one).astype(jnp.bfloat16)
    projected = jnp.einsum("ivd,sdh->sivh", first, w_qkv, preferred_element_type=jnp.float32)
    local_heads = w_qkv.shape[2] // HD
    heads_shape = (images, slots, local_heads, HD)
    queries = (projected[0] + b_qv[0]).astype(jnp.bfloat16).reshape(heads_shape)
    keyset = projected[1].astype(jnp.bfloat16).reshape(heads_shape)
    valueset = (projected[2] + b_qv[1]).astype(jnp.bfloat16).reshape(heads_shape)
    factor = HD ** (-0.5)
    key_visible = visible[:, None, None, :]

    def scores_of(query_part, key_part):
        raw_scores = (
            jnp.einsum("iqhe,ikhe->ihqk", query_part, key_part, preferred_element_type=jnp.float32)
            * factor
        )
        return jnp.where(key_visible, raw_scores, MASKED)

    scores = scores_of(queries, keyset)
    highest = jnp.max(scores, axis=-1, keepdims=True)
    logsum = highest + jnp.log(jnp.sum(jnp.exp(scores - highest), axis=-1, keepdims=True))
    attention = jnp.exp(scores - logsum).astype(jnp.bfloat16)
    attended = jnp.einsum(
        "ihqk,ikhe->iqhe", attention, valueset, preferred_element_type=jnp.float32
    )
    attended = attended.astype(jnp.bfloat16).reshape(images, slots, local_heads * HD)
    branch_part = jnp.einsum("ivc,cd->ivd", attended, w_out, preferred_element_type=jnp.float32)
    middle = tokens + lax.psum(branch_part, "tensor") + b_out
    middle_share = lax.dynamic_slice_in_dim(middle, begin, share, 0)
    second = affine_norm(middle, gain_two, shift_two).astype(jnp.bfloat16)
    inner = jnp.einsum("ivd,df->ivf", second, w_fc1, preferred_element_type=jnp.float32) + b_fc1
    hidden_values, gelu_back = jax.vjp(exact_gelu, inner)
    hidden = hidden_values.astype(jnp.bfloat16)
    mlp_part = jnp.einsum("ivf,fd->ivd", hidden, w_fc2, preferred_element_type=jnp.float32)
    mlp_share = lax.psum_scatter(
        mlp_part.astype(jnp.bfloat16), "tensor", scatter_dimension=0, tiled=True
    ).astype(jnp.float32)
    layer_out = ((middle_share + mlp_share + b_fc2) * mask_share).astype(jnp.bfloat16)
    grad_share = out_grad.astype(jnp.float32) * mask_share
    grad_b_fc2 = jnp.sum(grad_share, axis=(0, 1))
    grad_rows = lax.all_gather(grad_share.astype(jnp.bfloat16), "tensor", axis=0, tiled=True)
    grad_w_fc2 = jnp.einsum("ivf,ivd->fd", hidden, grad_rows, preferred_element_type=jnp.float32)
    grad_hidden = jnp.einsum("ivd,fd->ivf", grad_rows, w_fc2, preferred_element_type=jnp.float32)
    grad_inner = gelu_back(grad_hidden)[0].astype(jnp.bfloat16)
    grad_b_fc1 = jnp.sum(grad_inner, axis=(0, 1), dtype=jnp.float32)
    grad_w_fc1 = jnp.einsum("ivd,ivf->df", second, grad_inner, preferred_element_type=jnp.float32)
    second_part = jnp.einsum("ivf,df->ivd", grad_inner, w_fc1, preferred_element_type=jnp.float32)
    grad_second = lax.psum(second_part, "tensor")
    _, middle_back = jax.vjp(lambda inputs: affine_norm(inputs, gain_two, shift_two), middle)
    grad_middle = grad_rows.astype(jnp.float32) + middle_back(grad_second)[0]
    grad_second_share = lax.dynamic_slice_in_dim(grad_second, begin, share, 0)
    grad_gain_two = jnp.sum(grad_second_share * standard(middle_share), axis=(0, 1))
    grad_shift_two = jnp.sum(grad_second_share, axis=(0, 1))
    grad_middle_share = lax.dynamic_slice_in_dim(grad_middle, begin, share, 0)
    grad_middle_rows = grad_middle.astype(jnp.bfloat16)
    grad_b_out = jnp.sum(grad_middle_share, axis=(0, 1))
    grad_w_out = jnp.einsum(
        "ivc,ivd->cd", attended, grad_middle_rows, preferred_element_type=jnp.float32
    )
    grad_attended = jnp.einsum(
        "ivd,cd->ivc", grad_middle_rows, w_out, preferred_element_type=jnp.float32
    )
    grad_attended = grad_attended.astype(jnp.bfloat16).reshape(heads_shape)
    again = scores_of(queries, keyset)
    prob_exact = jnp.exp(again - logsum)
    prob_round = prob_exact.astype(jnp.bfloat16)
    grad_prob = jnp.einsum(
        "iqhe,ikhe->ihqk", grad_attended, valueset, preferred_element_type=jnp.float32
    )
    grad_scores = prob_exact * (grad_prob - jnp.sum(prob_exact * grad_prob, axis=-1, keepdims=True))
    grad_scores = grad_scores.astype(jnp.bfloat16)
    grad_queries = (
        jnp.einsum("ihqk,ikhe->iqhe", grad_scores, keyset, preferred_element_type=jnp.float32)
        * factor
    ).astype(jnp.bfloat16)
    grad_keys = (
        jnp.einsum("ihqk,iqhe->ikhe", grad_scores, queries, preferred_element_type=jnp.float32)
        * factor
    ).astype(jnp.bfloat16)
    grad_values = jnp.einsum(
        "ihqk,iqhe->ikhe", prob_round, grad_attended, preferred_element_type=jnp.float32
    ).astype(jnp.bfloat16)
    grad_projected = jnp.stack([grad_queries, grad_keys, grad_values]).reshape(
        3, images, slots, local_heads * HD
    )
    grad_b_qv = jnp.stack(
        [
            jnp.sum(grad_projected[0], axis=(0, 1), dtype=jnp.float32),
            jnp.sum(grad_projected[2], axis=(0, 1), dtype=jnp.float32),
        ]
    )
    grad_w_qkv = jnp.einsum(
        "ivd,sivh->sdh", first, grad_projected, preferred_element_type=jnp.float32
    )
    first_part = jnp.einsum(
        "sivh,sdh->ivd", grad_projected, w_qkv, preferred_element_type=jnp.float32
    )
    grad_first_share = lax.psum_scatter(first_part, "tensor", scatter_dimension=0, tiled=True)
    token_grad, grad_gain_one, grad_shift_one = norm_back(
        token_share, gain_one, shift_one, grad_first_share
    )
    grad_tokens = grad_middle_share + token_grad
    slot_share = lax.dynamic_slice_in_dim(keep_slots, begin, share, 0)
    image_rows = jnp.arange(share, dtype=jnp.int32)[:, None]
    grad_patches = (
        jnp.zeros((share, patches.shape[1], patches.shape[2]), jnp.float32)
        .at[image_rows, slot_share]
        .add(grad_tokens)
    )
    grad_w_qkv, grad_b_qv, grad_w_out, grad_w_fc1, grad_b_fc1, grad_w_fc2 = lax.psum(
        (grad_w_qkv, grad_b_qv, grad_w_out, grad_w_fc1, grad_b_fc1, grad_w_fc2), "dp"
    )
    grad_gain_one, grad_shift_one, grad_b_out, grad_gain_two, grad_shift_two, grad_b_fc2 = lax.psum(
        (grad_gain_one, grad_shift_one, grad_b_out, grad_gain_two, grad_shift_two, grad_b_fc2),
        ("dp", "tensor"),
    )
    return (
        layer_out,
        grad_patches,
        grad_gain_one,
        grad_shift_one,
        grad_w_qkv,
        grad_b_qv,
        grad_w_out,
        grad_b_out,
        grad_gain_two,
        grad_shift_two,
        grad_w_fc1,
        grad_b_fc1,
        grad_w_fc2,
        grad_b_fc2,
    )


def solution(mesh):
    return jax.shard_map(
        shards,
        mesh=mesh,
        in_specs=(
            P("dp", None, None),
            P("dp", None),
            P("dp"),
            P(),
            P(),
            P(None, None, "tensor"),
            P(None, "tensor"),
            P("tensor", None),
            P(),
            P(),
            P(),
            P(None, "tensor"),
            P("tensor"),
            P("tensor", None),
            P(),
            P(("dp", "tensor"), None, None),
        ),
        out_specs=(
            P(("dp", "tensor"), None, None),
            P(("dp", "tensor"), None, None),
            P(),
            P(),
            P(None, None, "tensor"),
            P(None, "tensor"),
            P("tensor", None),
            P(),
            P(),
            P(),
            P(None, "tensor"),
            P("tensor"),
            P("tensor", None),
            P(),
        ),
        check_vma=False,
    )
```

profile of v0, /device:TPU:0, one launch (start us, length us, event | category | flops | bytes accessed | tf_op | source)
XLA Modules:
  0.0 807.6 jit_solution(15770494399392824385)
XLA Ops:
  8.9 41.4 %gather_fusion = bf16[2352,768]{1,0:T(8,128)(2,1)} fusion(bf16[24,196,768]{2,0,1:T(8,128)(2,1)} %param.16, s32[2352]{0:T(1024)S(1)} %reshape.192), kind=kCustom, calls=%fused_computation | custom fusion | bytes 7244160 | tf_op jit(solution)/shard_map/jit(take_along_axis)/gather | solution.py:54
  50.3 5.8 reshape.195
  56.1 3.0 convert_reduce_fusion.3
  59.4 2.1 multiply_reduce_fusion.2
  61.6 3.3 convolution_bitcast_fusion.1
  64.9 1.8 fusion.58
  70.1 2.7 fusion.7
  74.3 1.6 copy-done.10
  78.4 4.3 fusion.36
  83.1 3.0 fusion.14
  86.2 141.4 %all-reduce.7.cloned.1.call-done = f32[24,98,768]{2,1,0:T(8,128)} async-done(((f32[24,98,768]{2,1,0:T(8,128)}), f32[24,98,768]{2,1,0:T(8,128)}) %all-reduce.7.cloned.1.call-update) | async-done | bytes 7225360 | tf_op jit(solution)/shard_map/psum | solution.py:82
  227.6 5.3 fusion.57
  236.0 6.4 convert_reduce_fusion.1
  242.5 3.0 copy-done.16
  245.5 18.4 %multiply_convert_fusion = (bf16[24,98,768]{2,1,0:T(8,128)(2,1)}, f32[24,98,768]{2,1,0:T(8,128)}) fusion(f32[24,98,768]{2,1,0:T(8,128)S(1)} %get-tuple-element.52, f32[768]{0:T(1024)S(1)} %copy-done.56, u32[98,768]{1,0:T(8,128)S(1)} %get-tuple-element.19, u32[98,768]{1,0:T(8,128)S(1)} %get-tuple-element.18), kind=kLoop, calls=%fused_computation.14 | loop fusion | flops 124637184 | bytes 18668544 | tf_op jit(solution)/shard_map/convert_element_type | solution.py:87
  263.9 11.6 %convert_reduce_fusion.2 = (f32[768]{0:T(1024)}, bf16[24,98,768]{2,1,0:T(8,128)(2,1)S(1)}) fusion(f32[24,98,768]{2,1,0:T(8,128)} %get-tuple-element.38, bf16[24,98,768]{2,1,0:T(8,128)(2,1)} %all-gather.2.cloned.1.call-done, bf16[768,768]{1,0:T(8,128)(2,1)} %param.29, f32[24,98,768]{2,1,0:T(8,128)} %copy-done.16, f32[768]{0:T(1024)} %param.28), kind=kOutput, calls=%fused_computation.10 | convolution fusion | flops 2805239040 | bytes 22861824 | tf_op jit(solution)/shard_map/ivd,fd->ivf/dot_general | solution.py:97
  275.5 1.8 copy-done.65
  277.3 15.7 %fusion.24 = f32[24,98,768]{2,1,0:T(8,128)} fusion(bf16[24,98,768]{2,1,0:T(8,128)(2,1)S(1)} %get-tuple-element.60, bf16[768,768]{1,0:T(8,128)(2,1)S(1)} %copy-done), kind=kOutput, calls=%fused_computation.83 | convolution fusion | flops 2774532096 | bytes 12017664 | tf_op jit(solution)/shard_map/ivf,df->ivd/dot_general | solution.py:101
  294.4 7.1 convolution_convert_fusion
  301.6 133.9 %all-reduce.9.cloned.1.call-done = f32[24,98,768]{2,1,0:T(8,128)} async-done(((f32[24,98,768]{2,1,0:T(8,128)}), f32[24,98,768]{2,1,0:T(8,128)}) %all-reduce.9.cloned.1.call-update) | async-done | bytes 7225360 | tf_op jit(solution)/shard_map/psum | solution.py:102
  435.5 6.4 multiply_reduce_fusion
  443.1 6.5 fusion.28
  450.6 2.9 add_add_fusion.1
  453.6 1.6 fusion.16
  455.2 2.3 copy-done.8
  459.2 2.1 multiply_reduce_fusion.3
  465.6 1.9 convert_reduce_fusion.4
  467.5 5.4 convolution_bitcast_fusion
  473.3 8.2 %convolution_bitcast_fusion.2 = f32[768,768]{1,0:T(8,128)} fusion(bf16[24,98,768]{2,1,0:T(8,128)(2,1)} %get-tuple-element.37, bf16[24,98,768]{2,1,0:T(8,128)(2,1)} %all-gather.2.cloned.1.call-done), kind=kOutput, calls=%fused_computation.73 | convolution fusion | flops 2774532096 | bytes 9584640 | tf_op jit(solution)/shard_map/ivf,ivd->fd/dot_general | solution.py:96
  481.5 8.8 %convolution_bitcast_fusion.3 = f32[768,768]{1,0:T(8,128)} fusion(bf16[24,98,768]{2,1,0:T(8,128)(2,1)S(1)} %copy-done.66, f32[24,98,768]{2,1,0:T(8,128)} %copy-done.2, f32[768]{0:T(1024)S(1)} %copy-done.62, f32[768]{0:T(1024)S(1)} %copy-done.42, f32[24,98]{1,0:T(8,128)S(1)} %copy-done.33, f32[24,98]{1,0:T(8,128)S(1)} %broadcast_multiply_fusion), kind=kOutput, calls=%fused_computation.74 | convolution fusion | flops 2783563776 | bytes 13222272 | tf_op jit(solution)/shard_map/ivd,ivf->df/dot_general | solution.py:100
  490.4 1.9 fusion.19
  494.9 5.7 convolution_bitcast_fusion.4
  501.4 2.7 fusion.9
  504.1 3.8 copy-done.9
  508.2 1.7 dynamic-slice_reduce_fusion.3
  509.9 1.9 multiply_reduce_fusion.5
  512.0 22.0 %all-reduce.1 = (f32[2,192]{1,0:T(2,128)}, f32[768]{0:T(1024)}) all-reduce(f32[2,192]{1,0:T(2,128)S(1)} %pad_maximum_fusion.3, f32[768]{0:T(1024)S(1)} %copy-done.58), channel_id=1, replica_groups=mesh['dp'=8,'tensor'=4] {'dp'}, use_global_device_ids=true, to_apply=%region_25.26 | all-reduce | flops 1152 | bytes 9216 | tf_op jit(solution)/shard_map/psum | solution.py:164
  534.0 3.9 dynamic-slice_reduce_fusion
  537.9 12.8 %reduce-scatter.5.cloned.1.call-done = f32[6,98,768]{2,1,0:T(8,128)} async-done(((f32[24,98,768]{2,1,0:T(8,128)}), f32[6,98,768]{2,1,0:T(8,128)}) %reduce-scatter.5.cloned.1.call-update) | async-done | bytes 1806352 | tf_op jit(solution)/shard_map/reduce_scatter | solution.py:152
  550.8 2.9 multiply_reduce_fusion.8
  553.7 2.4 multiply_reduce_fusion.6
  556.1 4.0 dynamic-slice_reduce_fusion.2
  560.2 1.6 reshape.200
  561.8 2.1 broadcast_in_dim.42
  564.0 81.2 %scatter_fusion = f32[6,196,768]{2,1,0:T(8,128)} fusion(f32[6,196,768]{2,1,0:T(8,128)} %broadcast_in_dim.42, s32[588]{0:T(1024)S(1)} %reshape.198, f32[588,768]{1,0:T(8,128)S(1)} %reshape.200), kind=kCustom, calls=%fused_computation.1 | custom fusion | flops 451584 | bytes 5423712 | tf_op jit(solution)/shard_map/scatter-add | solution.py:162
  645.2 41.1 %all-reduce = (f32[768]{0:T(1024)}, f32[768]{0:T(1024)}, f32[768]{0:T(1024)}, f32[768]{0:T(1024)}, f32[768]{0:T(1024)}, /*index=5*/f32[768]{0:T(1024)}) all-reduce(f32[768]{0:T(1024)S(1)} %get-tuple-element.14, f32[768]{0:T(1024)S(1)} %get-tuple-element.22, ...), channel_id=1, replica_groups=mesh['dp'=8,'tensor'=4] {'dp','tensor'}, use_global_device_ids=true, to_apply=%region_19.20 | all-reduce | flops 4608 | bytes 36864 | tf_op jit(solution)/shard_map/psum | solution.py:167
  686.3 107.5 %all-reduce.11.cloned.1.call-done = (f32[3,768,192]{1,2,0:T(8,128)}, f32[192,768]{1,0:T(8,128)}, f32[768,768]{1,0:T(8,128)}, f32[768,768]{1,0:T(8,128)}) async-done(((f32[3,768,192]{1,2,0:T(8,128)}, f32[192,768]{1,0:T(8,128)}, f32[768,768]{1,0:T(8,128)}, f32[768,768]{1,0:T(8,128)}), (f32[3,768,192]{1,2,0:T(8,128)}, f32[192,768]{1,0:T(8,128)}, f32[768,768]{1,0:T(8,128)}, ...) | async-done | bytes 7077904 | tf_op jit(solution)/shard_map/psum | solution.py:164
  793.8 2.9 copy.66
  (189 shorter events, 29.8 us)
Async XLA Ops:
  7.2 228.8 %copy-start = (bf16[768,768]{1,0:T(8,128)(2,1)S(1)}, bf16[768,768]{1,0:T(8,128)(2,1)}, u32[]{:S(2)}) copy-start(bf16[768,768]{1,0:T(8,128)(2,1)} %param.27) | copy-start | bytes 3538948
  7.2 220.4 %all-reduce.7.cloned.1.call-start = ((), (), s32[]{:S(2)}) async-start(), calls=%async_computation.2 | async-start | bytes 15335424 | tf_op jit(solution)/shard_map/psum | solution.py:82
  8.8 218.8 %copy-start.36 = (pred[24,98]{1,0:T(8,128)(4,1)}, pred[24,98]{1,0:T(8,128)(4,1)S(1)}, u32[]{:S(2)}) copy-start(pred[24,98]{1,0:T(8,128)(4,1)S(1)} %compare_and_fusion) | copy-start | bytes 7060
  56.1 5.4 copy-start.26
  56.1 5.4 copy-start.45
  56.1 5.4 copy-start.63
  59.4 5.5 copy-start.38
  68.6 5.7 copy-start.49
  70.1 4.1 copy-start.47
  72.8 4.5 copy-start.5
  74.2 4.2 copy-start.24
  82.7 144.8 %copy-start.55 = (f32[768]{0:T(1024)S(1)}, f32[768]{0:T(1024)}, u32[]{:S(2)}) copy-start(f32[768]{0:T(1024)} %param.24) | copy-start | bytes 9220
  82.7 181.2 %all-gather.2.cloned.1.call-start = ((), (), s32[]{:S(2)}) async-start(), calls=%async_computation.4 | async-start | bytes 4792320 | tf_op jit(solution)/shard_map/all_gather | solution.py:95
  83.1 149.8 %copy-start.43 = (f32[6,98]{1,0:T(8,128)}, f32[6,98]{1,0:T(8,128)S(1)}, u32[]{:S(2)}) copy-start(f32[6,98]{1,0:T(8,128)S(1)} %dynamic-slice_convert_fusion) | copy-start | bytes 7060
  86.1 349.4 %all-reduce.9.cloned.1.call-start = ((), (), s32[]{:S(2)}) async-start(), calls=%async_computation.5 | async-start | bytes 15335424 | tf_op jit(solution)/shard_map/psum | solution.py:102
  236.0 6.5 copy-start.31
  293.1 240.9 %reduce-scatter.3.cloned.1.call-start = ((), (), s32[]{:S(2)}) async-start(), calls=%async_computation.3 | async-start | bytes 4792320 | tf_op jit(solution)/shard_map/reduce_scatter | solution.py:89
  301.5 134.0 %copy-start.41 = (f32[768]{0:T(1024)S(1)}, f32[768]{0:T(1024)}, u32[]{:S(2)}) copy-start(f32[768]{0:T(1024)} %param.25) | copy-start | bytes 9220
  301.5 140.4 %copy-start.35 = (f32[24,98]{1,0:T(8,128)S(1)}, f32[24,98]{1,0:T(8,128)}, u32[]{:S(2)}) copy-start(f32[24,98]{1,0:T(8,128)} %copy-done.34) | copy-start | bytes 28228
  301.5 140.4 %copy-start.32 = (f32[24,98]{1,0:T(8,128)S(1)}, f32[24,98]{1,0:T(8,128)}, u32[]{:S(2)}) copy-start(f32[24,98]{1,0:T(8,128)} %copy-done.31) | copy-start | bytes 28228
  301.5 249.2 %reduce-scatter.5.cloned.1.call-start = ((), (), s32[]{:S(2)}) async-start(), calls=%async_computation.6 | async-start | bytes 9584640 | tf_op jit(solution)/shard_map/reduce_scatter | solution.py:152
  435.5 7.6 copy-start.7
  435.5 14.1 %slice-start = ((s8[7667712]{0:T(1024)(128)(4,1)}), s8[4194304]{0:T(1024)(128)(4,1)S(1)}, s32[]{:S(2)}) async-start(s8[7667712]{0:T(1024)(128)(4,1)} %bitcast.93), calls=%async_computation.8 | async-start | bytes 8388608
  443.1 6.5 slice-start.1
  443.1 7.5 copy-start.21
  453.5 4.9 copy-start.6
  453.5 5.7 copy-start.11
  453.5 5.6 copy-start.29
  453.6 5.6 copy-start.50
  465.5 7.4 copy-start.17
  473.0 8.5 %copy-start.33 = (f32[24,98]{1,0:T(8,128)S(1)}, f32[24,98]{1,0:T(8,128)}, u32[]{:S(2)}) copy-start(f32[24,98]{1,0:T(8,128)} %copy-done.31) | copy-start | bytes 28228
  473.0 8.5 %copy-start.42 = (f32[768]{0:T(1024)S(1)}, f32[768]{0:T(1024)}, u32[]{:S(2)}) copy-start(f32[768]{0:T(1024)} %param.25) | copy-start | bytes 9220
  473.0 8.5 %copy-start.62 = (f32[768]{0:T(1024)S(1)}, f32[768]{0:T(1024)}, u32[]{:S(2)}) copy-start(f32[768]{0:T(1024)} %param.26) | copy-start | bytes 9220
  473.0 320.7 %all-reduce.11.cloned.1.call-start = ((), (), s32[]{:S(2)}) async-start(), calls=%async_computation.7 | async-start | bytes 14155776 | tf_op jit(solution)/shard_map/psum | solution.py:164
  473.3 8.2 %copy-start.66 = (bf16[24,98,768]{2,1,0:T(8,128)(2,1)S(1)}, bf16[24,98,768]{2,1,0:T(8,128)(2,1)}, u32[]{:S(2)}) copy-start(bf16[24,98,768]{2,1,0:T(8,128)(2,1)} %copy-done.65) | copy-start | bytes 10838020
  473.3 17.0 %slice-start.2 = ((s8[7667712]{0:T(1024)(128)(4,1)}), s8[4194304]{0:T(1024)(128)(4,1)S(1)}, s32[]{:S(2)}) async-start(s8[7667712]{0:T(1024)(128)(4,1)} %bitcast.95), calls=%async_computation.10 | async-start | bytes 8388608
  481.5 8.8 %slice-start.3 = ((s8[7667712]{0:T(1024)(128)(4,1)}), s8[3473408]{0:T(1024)(128)(4,1)S(1)}, s32[]{:S(2)}) async-start(s8[7667712]{0:T(1024)(128)(4,1)} %bitcast.95), calls=%async_computation.11 | async-start | bytes 6946816
  481.5 8.8 %copy-start.14 = (bf16[24,3,64,98]{3,2,1,0:T(8,128)(2,1)S(1)}, bf16[24,3,64,98]{3,2,1,0:T(8,128)(2,1)}, u32[]{:S(2)}) copy-start(bf16[24,3,64,98]{3,2,1,0:T(8,128)(2,1)} %copy-done.13) | copy-start | bytes 2709508
  490.4 4.5 copy-start.20
  490.4 4.5 copy-start.37
  490.4 4.5 copy-start.39
  490.4 4.5 copy-start.46
  490.4 4.5 copy-start.53
  490.4 4.5 copy-start.64
  507.9 26.0 %copy-start.44 = (f32[6,98]{1,0:T(8,128)S(1)}, f32[6,98]{1,0:T(8,128)}, u32[]{:S(2)}) copy-start(f32[6,98]{1,0:T(8,128)} %copy-done.43) | copy-start | bytes 7060
  507.9 26.0 %copy-start.57 = (f32[768]{0:T(1024)S(1)}, f32[768]{0:T(1024)}, u32[]{:S(2)}) copy-start(f32[768]{0:T(1024)} %param.30) | copy-start | bytes 9220
  563.9 81.2 %copy-start.51 = (f32[768]{0:T(1024)S(1)}, f32[768]{0:T(1024)}, u32[]{:S(2)}) copy-start(f32[768]{0:T(1024)} %get-tuple-element.46) | copy-start | bytes 9220
  793.8 5.2 copy-start.22
  (29 other events, 83.6 us)
Sparse Core Ops, SparseCore 0:
  82.9 144.6 all-reduce.6
  229.8 32.6 all-gather.1
  293.2 142.2 all-reduce.8
  437.9 42.5 reduce-scatter.2
  483.0 67.6 reduce-scatter.4
  556.2 237.5 all-reduce.10
where the time goes:
time: 820 us; the launch traced here: 808 us
  waiting for transfers between devices  396 us (48%)
  other arithmetic  156 us (19%)
  matrix products  91 us (11%)
  local copies, waits for them, and re-layouts  85.9 us (10%)
  blocking collectives  63.1 us (8%)
  between operations  15.4 us (2%)
    psum x1, waiting for transfers between devices, shards(): middle = tokens + lax.psum(branch_part, 'tensor') + b_out  141 us
    psum x1, waiting for transfers between devices, shards(): grad_second = lax.psum(second_part, 'tensor')  134 us
    psum x1, waiting for transfers between devices, shards(): lax.psum((grad_w_qkv, grad_b_qv, grad_w_out, grad_w_fc1, grad_b_fc1, grad...  107 us
    scatter-add x1, other arithmetic, shards(): grad_patches = jnp.zeros((share, patches.shape[1], patches.shape[2]), jnp...  81.2 us
    gather x3, local copies, waits for them, and re-layouts, shards(): jnp.take_along_axis(patches, keep_slots[:, :, None], axis=1)  47.4 us
    psum x1, blocking collectives, shards(): lax.psum((grad_gain_one, grad_shift_one, grad_b_out, grad_gain_two, grad_...  41.1 us
    unnamed x146, local copies, waits for them, and re-layouts  30.1 us
    psum x1, blocking collectives, shards(): lax.psum((grad_w_qkv, grad_b_qv, grad_w_out, grad_w_fc1, grad_b_fc1, grad...  22 us
  transfers between devices with their start and end apart: 6, of which 4 were waited for; matrix products, arithmetic and copies ran while one was open for 25% of the time, Pallas kernels for 0%

commit v1 on v0

--- a/solution.py
+++ b/solution.py
@@ -99,7 +99,14 @@
     grad_b_fc1 = jnp.sum(grad_inner, axis=(0, 1), dtype=jnp.float32)
     grad_w_fc1 = jnp.einsum("ivd,ivf->df", second, grad_inner, preferred_element_type=jnp.float32)
     second_part = jnp.einsum("ivf,df->ivd", grad_inner, w_fc1, preferred_element_type=jnp.float32)
-    grad_second = lax.psum(second_part, "tensor")
+    n_shards = lax.axis_size("tensor")
+    grad_second, local_part = (second_part, 0)
+    while 1 << local_part < n_shards:
+        k_now = lax.ppermute(
+            grad_second, "tensor", perm=tuple(((u, u ^ 1 << local_part) for u in range(n_shards)))
+        )
+        grad_second = grad_second + k_now
+        local_part = local_part + 1
     _, middle_back = jax.vjp(lambda inputs: affine_norm(inputs, gain_two, shift_two), middle)
     grad_middle = grad_rows.astype(jnp.float32) + middle_back(grad_second)[0]
     grad_second_share = lax.dynamic_slice_in_dim(grad_second, begin, share, 0)

time: 820 us -> 871 us (1.062)
  waiting for transfers between devices: 396 us -> 437 us
  other arithmetic: 156 us -> 171 us
  matrix products: 91 us -> 80.2 us
    ppermute x0 -> x2, waiting for transfers between devices: none -> 185 us  [shards(): lax.ppermute(grad_second, 'tensor', perm=tuple(((u, u ^ 1 << local_part)...]
    psum x1 -> x0, waiting for transfers between devices: 134 us -> none  [shards(): grad_second = lax.psum(second_part, 'tensor')]
    dot_general x1, matrix products: 15.7 us -> 3.22 us  [shards(): jnp.einsum('ivf,df->ivd', grad_inner, w_fc1, preferred_element_type=jnp.f...]
    reduce_scatter x1, waiting for transfers between devices: 12.8 us -> 3.52 us  [shards(): lax.psum_scatter(first_part, 'tensor', scatter_dimension=0, tiled=True)]
  transfers between devices with their start and end apart: 6 -> 7, of which waited for: 4 -> 5; matrix products, arithmetic and copies ran while one was open for 25% -> 24% of each run, Pallas kernels for 0% -> 0%
where the time goes in v1:
time: 871 us; the launch traced here: 858 us
  waiting for transfers between devices  437 us (50%)
  other arithmetic  171 us (20%)
  local copies, waits for them, and re-layouts  90 us (10%)
  matrix products  80.2 us (9%)
  blocking collectives  63.5 us (7%)
  between operations  14.9 us (2%)
    ppermute x2, waiting for transfers between devices, shards(): lax.ppermute(grad_second, 'tensor', perm=tuple(((u, u ^ 1 << local_part)...  185 us
    psum x1, waiting for transfers between devices, shards(): middle = tokens + lax.psum(branch_part, 'tensor') + b_out  141 us
    psum x1, waiting for transfers between devices, shards(): lax.psum((grad_w_qkv, grad_b_qv, grad_w_out, grad_w_fc1, grad_b_fc1, grad...  108 us
    scatter-add x1, other arithmetic, shards(): grad_patches = jnp.zeros((share, patches.shape[1], patches.shape[2]), jnp...  81.2 us
    gather x3, local copies, waits for them, and re-layouts, shards(): jnp.take_along_axis(patches, keep_slots[:, :, None], axis=1)  47.4 us
    psum x1, blocking collectives, shards(): lax.psum((grad_gain_one, grad_shift_one, grad_b_out, grad_gain_two, grad_...  41.2 us
    unnamed x146, local copies, waits for them, and re-layouts  26.4 us
    psum x1, blocking collectives, shards(): lax.psum((grad_w_qkv, grad_b_qv, grad_w_out, grad_w_fc1, grad_b_fc1, grad...  22.2 us
  transfers between devices with their start and end apart: 7, of which 5 were waited for; matrix products, arithmetic and copies ran while one was open for 24% of the time, Pallas kernels for 0%

profile of v1, /device:TPU:0, one launch (start us, length us, event | category | flops | bytes accessed | tf_op | source)
XLA Modules:
  0.0 858.3 jit_solution(10286286334301651477)
XLA Ops:
  8.9 41.4 %gather_fusion = bf16[2352,768]{1,0:T(8,128)(2,1)} fusion(bf16[24,196,768]{2,0,1:T(8,128)(2,1)} %param.16, s32[2352]{0:T(1024)S(1)} %reshape.192), kind=kCustom, calls=%fused_computation | custom fusion | bytes 7244160 | tf_op jit(solution)/shard_map/jit(take_along_axis)/gather | solution.py:54
  50.3 5.9 reshape.195
  56.2 3.0 convert_reduce_fusion.3
  59.4 2.1 multiply_reduce_fusion.2
  61.6 3.3 convolution_bitcast_fusion.1
  69.4 2.7 fusion.7
  72.1 1.9 copy-done.5
  76.1 4.1 convolution_convert_fusion.2
  81.2 4.3 fusion.36
  86.1 3.0 fusion.14
  89.2 141.2 %all-reduce.6.cloned.1.call-done = f32[24,98,768]{2,1,0:T(8,128)} async-done(((f32[24,98,768]{2,1,0:T(8,128)}), f32[24,98,768]{2,1,0:T(8,128)}) %all-reduce.6.cloned.1.call-update) | async-done | bytes 7225360 | tf_op jit(solution)/shard_map/psum | solution.py:82
  230.4 5.3 fusion.57
  238.8 6.4 convert_reduce_fusion.1
  245.3 3.0 copy-done.17
  248.3 18.5 %multiply_convert_fusion = (bf16[24,98,768]{2,1,0:T(8,128)(2,1)}, f32[24,98,768]{2,1,0:T(8,128)}) fusion(f32[24,98,768]{2,1,0:T(8,128)S(1)} %get-tuple-element.54, f32[768]{0:T(1024)S(1)} %copy-done.57, u32[98,768]{1,0:T(8,128)S(1)} %get-tuple-element.19, u32[98,768]{1,0:T(8,128)S(1)} %get-tuple-element.18), kind=kLoop, calls=%fused_computation.16 | loop fusion | flops 124637184 | bytes 18668544 | tf_op jit(solution)/shard_map/convert_element_type | solution.py:87
  266.8 11.8 %convert_reduce_fusion.2 = (f32[768]{0:T(1024)}, bf16[24,98,768]{2,1,0:T(8,128)(2,1)S(1)}) fusion(f32[24,98,768]{2,1,0:T(8,128)} %get-tuple-element.40, bf16[24,98,768]{2,1,0:T(8,128)(2,1)} %all-gather.2.cloned.1.call-done, bf16[768,768]{1,0:T(8,128)(2,1)} %param.29, f32[24,98,768]{2,1,0:T(8,128)} %copy-done.17, f32[768]{0:T(1024)} %param.28), kind=kOutput, calls=%fused_computation.12 | convolution fusion | flops 2805239040 | bytes 22861824 | tf_op jit(solution)/shard_map/ivd,fd->ivf/dot_general | solution.py:97
  280.4 3.2 fusion.24
  283.7 2.3 copy.47
  286.8 11.6 %collective-permute-done = f32[24,98,768]{2,0,1:T(8,128)} collective-permute-done((f32[24,98,768]{2,0,1:T(8,128)S(1)}, f32[24,98,768]{2,0,1:T(8,128)}, u32[]{:S(2)}, u32[]{:S(2)}) %collective-permute-start) | collective-permute-done | bytes 7225376 | tf_op jit(solution)/shard_map/ppermute | solution.py:105
  298.4 7.8 copy_add_fusion.1
  306.2 5.5 copy.49
  313.4 4.6 convolution_convert_fusion
  318.0 173.2 %collective-permute-done.1 = f32[24,98,768]{2,0,1:T(8,128)} collective-permute-done((f32[24,98,768]{2,0,1:T(8,128)}, f32[24,98,768]{2,0,1:T(8,128)}, u32[]{:S(2)}, u32[]{:S(2)}) %collective-permute-start.1) | collective-permute-done | bytes 7225376 | tf_op jit(solution)/shard_map/ppermute | solution.py:105
  491.2 9.5 %multiply_reduce_fusion = (f32[24,98]{1,0:T(8,128)S(1)}, f32[24,98,768]{2,1,0:T(8,128)S(1)}) fusion(f32[24,98,768]{2,1,0:T(8,128)} %copy-done.2, f32[768]{0:T(1024)S(1)} %copy-done.46, f32[24,98]{1,0:T(8,128)S(1)} %broadcast_multiply_fusion, f32[24,98,768]{2,1,0:T(8,128)} %copy-done.9, f32[24,98,768]{2,0,1:T(8,128)} %collective-permute-done.1), kind=kLoop, calls=%fused_computation.14 | loop fusion | flops 9029328 | bytes 28923264 | tf_op jit(solution)/shard_map/transpose(jvp())/reduce_sum | solution.py:15
  500.8 7.6 fusion.28
  508.5 5.5 add_add_fusion.1
  515.6 2.2 copy-done.7
  519.5 2.1 multiply_reduce_fusion.3
  525.9 2.0 convert_reduce_fusion.4
  527.9 5.4 convolution_bitcast_fusion
  533.9 8.1 convolution_bitcast_fusion.2
  542.0 10.3 %convolution_bitcast_fusion.3 = f32[768,768]{1,0:T(8,128)} fusion(bf16[24,98,768]{2,1,0:T(8,128)(2,1)S(1)} %copy-done.68, f32[24,98,768]{2,1,0:T(8,128)} %copy-done.2, f32[768]{0:T(1024)S(1)} %copy-done.64, f32[768]{0:T(1024)S(1)} %copy-done.47, f32[24,98]{1,0:T(8,128)S(1)} %copy-done.34, f32[24,98]{1,0:T(8,128)S(1)} %broadcast_multiply_fusion), kind=kOutput, calls=%fused_computation.76 | convolution fusion | flops 2783563776 | bytes 13222272 | tf_op jit(solution)/shard_map/ivd,ivf->df/dot_general | solution.py:100
  552.4 1.9 fusion.19
  555.4 5.7 convolution_bitcast_fusion.4
  561.9 2.6 fusion.9
  564.5 3.1 copy-done.10
  569.6 2.0 multiply_reduce_fusion.5
  571.8 22.2 %all-reduce.1 = (f32[2,192]{1,0:T(2,128)}, f32[768]{0:T(1024)}) all-reduce(f32[2,192]{1,0:T(2,128)S(1)} %pad_maximum_fusion.3, f32[768]{0:T(1024)S(1)} %copy-done.59), channel_id=1, replica_groups=mesh['dp'=8,'tensor'=4] {'dp'}, use_global_device_ids=true, to_apply=%region_24.25 | all-reduce | flops 1152 | bytes 9216 | tf_op jit(solution)/shard_map/psum | solution.py:171
  594.0 3.9 dynamic-slice_reduce_fusion
  598.0 3.5 reduce-scatter.5.cloned.1.call-done
  601.5 2.9 multiply_reduce_fusion.8
  604.4 2.4 multiply_reduce_fusion.6
  606.9 4.0 dynamic-slice_reduce_fusion.2
  612.5 2.1 broadcast_in_dim.42
  614.6 81.2 %scatter_fusion = f32[6,196,768]{2,1,0:T(8,128)} fusion(f32[6,196,768]{2,1,0:T(8,128)} %broadcast_in_dim.42, s32[588]{0:T(1024)S(1)} %reshape.198, f32[588,768]{1,0:T(8,128)S(1)} %reshape.200), kind=kCustom, calls=%fused_computation.1 | custom fusion | flops 451584 | bytes 5423712 | tf_op jit(solution)/shard_map/scatter-add | solution.py:169
  695.8 41.2 %all-reduce = (f32[768]{0:T(1024)}, f32[768]{0:T(1024)}, f32[768]{0:T(1024)}, f32[768]{0:T(1024)}, f32[768]{0:T(1024)}, /*index=5*/f32[768]{0:T(1024)}) all-reduce(f32[768]{0:T(1024)S(1)} %get-tuple-element.14, f32[768]{0:T(1024)S(1)} %get-tuple-element.22, ...), channel_id=1, replica_groups=mesh['dp'=8,'tensor'=4] {'dp','tensor'}, use_global_device_ids=true, to_apply=%region_18.19 | all-reduce | flops 4608 | bytes 36864 | tf_op jit(solution)/shard_map/psum | solution.py:174
  737.1 107.9 %all-reduce.8.cloned.1.call-done = (f32[3,768,192]{1,2,0:T(8,128)}, f32[192,768]{1,0:T(8,128)}, f32[768,768]{1,0:T(8,128)}, f32[768,768]{1,0:T(8,128)}) async-done(((f32[3,768,192]{1,2,0:T(8,128)}, f32[192,768]{1,0:T(8,128)}, f32[768,768]{1,0:T(8,128)}, f32[768,768]{1,0:T(8,128)}), (f32[3,768,192]{1,2,0:T(8,128)}, f32[192,768]{1,0:T(8,128)}, f32[768,768]{1,0:T(8,128)}, ...) | async-done | bytes 7077904 | tf_op jit(solution)/shard_map/psum | solution.py:171
  845.0 2.9 copy.72
  (192 shorter events, 34.6 us)
Async XLA Ops:
  7.2 231.6 %copy-start = (bf16[768,768]{1,0:T(8,128)(2,1)S(1)}, bf16[768,768]{1,0:T(8,128)(2,1)}, u32[]{:S(2)}) copy-start(bf16[768,768]{1,0:T(8,128)(2,1)} %param.27) | copy-start | bytes 3538948
  7.2 223.2 %all-reduce.6.cloned.1.call-start = ((), (), s32[]{:S(2)}) async-start(), calls=%async_computation.2 | async-start | bytes 15335424 | tf_op jit(solution)/shard_map/psum | solution.py:82
  8.8 221.6 %copy-start.37 = (pred[24,98]{1,0:T(8,128)(4,1)}, pred[24,98]{1,0:T(8,128)(4,1)S(1)}, u32[]{:S(2)}) copy-start(pred[24,98]{1,0:T(8,128)(4,1)S(1)} %compare_and_fusion) | copy-start | bytes 7060
  56.1 5.4 copy-start.28
  56.1 5.4 copy-start.43
  56.1 5.4 copy-start.65
  59.4 5.5 copy-start.39
  69.4 6.0 copy-start.48
  76.1 9.4 %copy-start.50 = (f32[3,64]{1,0:T(4,128)}, f32[3,64]{1,0:T(4,128)S(1)}, u32[]{:S(2)}) copy-start(f32[3,64]{1,0:T(4,128)S(1)} %add.186) | copy-start | bytes 2308
  76.1 5.1 copy-start.26
  85.5 144.8 %copy-start.56 = (f32[768]{0:T(1024)S(1)}, f32[768]{0:T(1024)}, u32[]{:S(2)}) copy-start(f32[768]{0:T(1024)} %param.24) | copy-start | bytes 9220
  85.6 181.3 %all-gather.2.cloned.1.call-start = ((), (), s32[]{:S(2)}) async-start(), calls=%async_computation.4 | async-start | bytes 4792320 | tf_op jit(solution)/shard_map/all_gather | solution.py:95
  86.1 149.6 %copy-start.41 = (f32[6,98]{1,0:T(8,128)}, f32[6,98]{1,0:T(8,128)S(1)}, u32[]{:S(2)}) copy-start(f32[6,98]{1,0:T(8,128)S(1)} %dynamic-slice_convert_fusion) | copy-start | bytes 7060
  89.2 504.9 %reduce-scatter.3.cloned.1.call-start = ((), (), s32[]{:S(2)}) async-start(), calls=%async_computation.3 | async-start | bytes 4792320 | tf_op jit(solution)/shard_map/reduce_scatter | solution.py:89
  238.8 6.5 copy-start.32
  286.8 11.6 %collective-permute-start = (f32[24,98,768]{2,0,1:T(8,128)S(1)}, f32[24,98,768]{2,0,1:T(8,128)}, u32[]{:S(2)}, u32[]{:S(2)}) collective-permute-start(f32[24,98,768]{2,0,1:T(8,128)S(1)} %copy.47), channel_id=1, source_target_pairs={{0,1},{1,0},{2,3},{3,2},{4,5},{5,4},{6,7},{7,6},{8,9},{9,8},{10,11... | collective-permute-start | bytes 21676040 | tf_op jit(solution)/shard_map/ppermute | solution.py:105
  306.2 6.5 copy-start.9
  306.2 7.1 copy-start.23
  306.2 7.1 copy-start.62
  312.8 178.4 %collective-permute-start.1 = (f32[24,98,768]{2,0,1:T(8,128)}, f32[24,98,768]{2,0,1:T(8,128)}, u32[]{:S(2)}, u32[]{:S(2)}) collective-permute-start(f32[24,98,768]{2,0,1:T(8,128)} %copy.49), channel_id=1, source_target_pairs={{0,2},{1,3},{2,0},{3,1},{4,6},{5,7},{6,4},{7,5},{8,10},{9,11},{10,... | collective-permute-start | bytes 21676040 | tf_op jit(solution)/shard_map/ppermute | solution.py:105
  317.9 173.3 %copy-start.46 = (f32[768]{0:T(1024)S(1)}, f32[768]{0:T(1024)}, u32[]{:S(2)}) copy-start(f32[768]{0:T(1024)} %param.25) | copy-start | bytes 9220
  318.0 182.8 %copy-start.36 = (f32[24,98]{1,0:T(8,128)S(1)}, f32[24,98]{1,0:T(8,128)}, u32[]{:S(2)}) copy-start(f32[24,98]{1,0:T(8,128)} %copy-done.35) | copy-start | bytes 28228
  318.0 182.8 %copy-start.33 = (f32[24,98]{1,0:T(8,128)S(1)}, f32[24,98]{1,0:T(8,128)}, u32[]{:S(2)}) copy-start(f32[24,98]{1,0:T(8,128)} %copy-done.32) | copy-start | bytes 28228
  318.0 283.5 %reduce-scatter.5.cloned.1.call-start = ((), (), s32[]{:S(2)}) async-start(), calls=%async_computation.5 | async-start | bytes 9584640 | tf_op jit(solution)/shard_map/reduce_scatter | solution.py:159
  500.7 7.7 copy-start.8
  500.8 7.7 copy-start.22
  508.5 5.5 copy-start.27
  513.9 3.9 copy-start.7
  514.0 4.9 copy-start.6
  514.0 5.6 copy-start.12
  514.0 5.6 copy-start.30
  514.0 5.6 copy-start.51
  525.9 7.4 copy-start.18
  533.4 8.6 %copy-start.34 = (f32[24,98]{1,0:T(8,128)S(1)}, f32[24,98]{1,0:T(8,128)}, u32[]{:S(2)}) copy-start(f32[24,98]{1,0:T(8,128)} %copy-done.32) | copy-start | bytes 28228
  533.4 8.6 copy-start.47
  533.4 8.6 copy-start.64
  533.4 311.6 %all-reduce.8.cloned.1.call-start = ((), (), s32[]{:S(2)}) async-start(), calls=%async_computation.6 | async-start | bytes 14155776 | tf_op jit(solution)/shard_map/psum | solution.py:171
  533.9 8.1 copy-start.68
  533.9 18.5 %slice-start = ((s8[7667712]{0:T(1024)(128)(4,1)}), s8[4194304]{0:T(1024)(128)(4,1)S(1)}, s32[]{:S(2)}) async-start(s8[7667712]{0:T(1024)(128)(4,1)} %bitcast.93), calls=%async_computation.7 | async-start | bytes 8388608
  542.0 10.4 %slice-start.1 = ((s8[7667712]{0:T(1024)(128)(4,1)}), s8[3473408]{0:T(1024)(128)(4,1)S(1)}, s32[]{:S(2)}) async-start(s8[7667712]{0:T(1024)(128)(4,1)} %bitcast.93), calls=%async_computation.8 | async-start | bytes 6946816
  542.0 10.4 %copy-start.15 = (bf16[24,3,64,98]{3,2,1,0:T(8,128)(2,1)S(1)}, bf16[24,3,64,98]{3,2,1,0:T(8,128)(2,1)}, u32[]{:S(2)}) copy-start(bf16[24,3,64,98]{3,2,1,0:T(8,128)(2,1)} %copy-done.14) | copy-start | bytes 2709508
  567.6 3.9 copy-start.55
  567.6 4.1 copy-start.59
  567.6 26.4 %copy-start.42 = (f32[6,98]{1,0:T(8,128)S(1)}, f32[6,98]{1,0:T(8,128)}, u32[]{:S(2)}) copy-start(f32[6,98]{1,0:T(8,128)} %copy-done.41) | copy-start | bytes 7060
  567.6 26.4 %copy-start.58 = (f32[768]{0:T(1024)S(1)}, f32[768]{0:T(1024)}, u32[]{:S(2)}) copy-start(f32[768]{0:T(1024)} %param.30) | copy-start | bytes 9220
  614.6 81.2 %copy-start.52 = (f32[768]{0:T(1024)S(1)}, f32[768]{0:T(1024)}, u32[]{:S(2)}) copy-start(f32[768]{0:T(1024)} %get-tuple-element.48) | copy-start | bytes 9220
  845.0 3.8 copy-start.25
  845.0 5.2 copy-start.24
  (30 other events, 80.2 us)
Sparse Core Ops, SparseCore 0:
  85.7 144.6 all-reduce.5
  232.6 32.6 all-gather.1
  318.1 63.7 reduce-scatter.2
  533.5 67.9 reduce-scatter.4
  607.5 237.4 all-reduce.7
